TPU v7x, 32 devices: a whole 2x2x4 slice. The times are simulated.
32 devices in a mesh: prompt: 4 (over y, x), sample: 8 (over z, core).
Axes of the slice: x: 2, y: 2, z: 4, core: 2. Of those that a mesh axis runs over, the one named last changes fastest.
Arguments:
- embeddings: bfloat16 [32, 512, 1024], P(('prompt', 'sample')), parts along dimension 0
- lengths: int32 [32], P(('prompt', 'sample')), parts along dimension 0, may hold values from 32 to 512, as said below
Outputs:
- precision: float32 [32, 8], P(('prompt', 'sample')), parts along dimension 0
- utility: float32 [32], P(('prompt', 'sample')), parts along dimension 0
There are 4 independent parts, one for each index of `prompt`. A program takes and returns all parts, laid end to end along the dimension named above; each array names one. Nothing has to cross between parts.
Inputs may be any that keep to these rules, and one draw needn't show every extreme that they name: `lengths`: some sample of the prompt has exactly 512 tokens.
All inputs are finite; a program needn't handle non-finite values.
Results may differ from a plain program's by a relative error of at most 0.0007.
Values may be sent and summed in bfloat16 or wider, within the bound.
A program may use at most 128 MiB of HBM per device.

v0:
```python
import jax
import jax.numpy as jnp
from jax import lax
from jax.sharding import PartitionSpec as P


def tile_pairs(own, own_len, other, other_len):
    similar = jnp.einsum("aie,bje->abij", own, other, preferred_element_type=jnp.float32)
    places = jnp.arange(own.shape[1], dtype=jnp.int32)
    own_ok = places[None, :] < own_len[:, None]
    other_ok = places[None, :] < other_len[:, None]
    masked = jnp.where(other_ok[None, :, None, :], similar, jnp.float32(-4.0))
    best_row = jnp.max(masked, axis=3)
    forward = jnp.sum(jnp.where(own_ok[:, None, :], best_row, jnp.float32(0.0)), axis=2)
    forward = forward / own_len[:, None].astype(jnp.float32)
    masked_col = jnp.where(own_ok[:, None, :, None], similar, jnp.float32(-4.0))
    best_col = jnp.max(masked_col, axis=2)
    backward = jnp.sum(jnp.where(other_ok[None, :, :], best_col, jnp.float32(0.0)), axis=2)
    backward = backward / other_len[None, :].astype(jnp.float32)
    return (forward, backward)


def body(embeddings, lengths):
    values = embeddings.astype(jnp.float32)
    unit = (values / jnp.sqrt(jnp.sum(values * values, axis=2, keepdims=True) + 1e-06)).astype(
        jnp.bfloat16
    )
    devices = lax.axis_size("sample")
    here = lax.axis_index("sample")
    per_dev = unit.shape[0]
    total = per_dev * devices
    base = here * per_dev
    piece = lax.all_gather(unit, "sample", axis=0, tiled=True)
    piece_len = lax.all_gather(lengths, "sample", axis=0, tiled=True)
    ahead, behind = tile_pairs(unit, lengths, piece, piece_len)
    own_index = base + jnp.arange(per_dev, dtype=jnp.int32)
    offdiag = jnp.arange(total, dtype=jnp.int32)[None, :] != own_index[:, None]
    utility = jnp.sum(jnp.where(offdiag, ahead + behind, jnp.float32(0.0)), axis=1)
    utility = utility / jnp.float32(2 * (total - 1))
    return (ahead, utility)


def solution(mesh):
    in_specs = (P(("prompt", "sample"), None, None), P(("prompt", "sample")))
    out_specs = (P(("prompt", "sample"), None), P(("prompt", "sample")))
    return jax.shard_map(body, mesh=mesh, in_specs=in_specs, out_specs=out_specs, check_vma=False)
```

profile of v0, /device:TPU:0, one launch (start us, length us, event | category | flops | bytes accessed | tf_op | source)
XLA Modules:
  0.0 114.2 jit_solution(15194973884810265625)
XLA Ops:
  7.2 0.0 all-gather.2.cloned.1.call-start
  7.2 1.5 %fusion.2 = f32[512]{0:T(512)S(1)} fusion(bf16[1,512,1024]{2,1,0:T(8,128)(2,1)} %param.2), kind=kLoop, calls=%fused_computation.6 | loop fusion | flops 1572352 | bytes 1050624 | tf_op jit(solution)/shard_map/reduce_sum | solution.py:25
  8.7 2.6 %fusion.3 = bf16[1,512,1024]{2,1,0:T(8,128)(2,1)} fusion(bf16[1,512,1024]{2,1,0:T(8,128)(2,1)} %param.2, f32[512]{0:T(512)S(1)} %add_sqrt_fusion), kind=kLoop, calls=%fused_computation.7 | loop fusion | flops 1572864 | bytes 2099200 | tf_op jit(solution)/shard_map/convert_element_type | solution.py:25
  11.4 0.0 all-gather.2.cloned.1.call-update
  12.1 1.2 %dynamic-slice = u32[1]{0:T(128)} dynamic-slice(u32[32]{0:T(128)} %constant.20, u32[]{:T(128)S(6)} %add.18), dynamic_slice_sizes={1} | dynamic-slice | bytes 12
  13.3 0.8 dynamic-update-slice
  14.1 10.6 %all-reduce = s32[8]{0:T(128)S(1)} all-reduce(s32[8]{0:T(128)S(1)} %dynamic-update-slice), channel_id=1, replica_groups=mesh['prompt'=4,'sample'=8] {'sample'}, use_global_device_ids=true, to_apply=%add | all-reduce | flops 8 | bytes 64
  24.7 0.1 iota_compare_fusion
  24.8 71.5 %all-gather.2.cloned.1.call-done = bf16[8,512,1024]{2,1,0:T(8,128)(2,1)} async-done(((bf16[1,512,1024]{2,1,0:T(8,128)(2,1)}), bf16[8,512,1024]{2,1,0:T(8,128)(2,1)}) %all-gather.2.cloned.1.call-update) | async-done | bytes 8388624 | tf_op jit(solution)/shard_map/all_gather | solution.py:33
  96.3 7.9 %fusion.1 = (f32[8,512]{1,0:T(8,128)S(1)}, f32[8,512]{1,0:T(8,128)S(1)}) fusion(pred[512]{0:T(512)(128)(4,1)S(1)} %iota_compare_fusion.1, pred[8,512]{1,0:T(8,128)(4,1)S(1)} %iota_compare_fusion, bf16[8,512,1024]{2,1,0:T(8,128)(2,1)} %all-gather.2.cloned.1.call-done, bf16[1,512,1024]{2,1,0:T(8,128)(2,1)} %fusion.3), kind=kOutput, calls=%fused_computation.3 | convolution fusion | flops 4303347712 | bytes 9474560 | tf_op jit(solution)/shard_map/aie,bje->abij/dot_general | solution.py:8
  104.3 0.2 select_reduce_fusion
  104.4 1.1 fusion.6
  (3 shorter events, 0.0 us)
Async XLA Ops:
  7.2 89.1 %all-gather.2.cloned.1.call-start = ((), (), s32[]{:S(2)}) async-start(), calls=%async_computation | async-start | bytes 9437184 | tf_op jit(solution)/shard_map/all_gather | solution.py:33
Sparse Core Ops, SparseCore 0:
  11.5 84.7 all-gather.1
where the time goes:
time: 114 us
  waiting for transfers between devices  71.5 us (63%)
  between operations  16.5 us (14%)
  blocking collectives  10.6 us (9%)
  matrix products  7.94 us (7%)
  other arithmetic  5.55 us (5%)
  local copies, waits for them, and re-layouts  2 us (2%)
    all_gather x1, waiting for transfers between devices, body(): piece = lax.all_gather(unit, 'sample', axis=0, tiled=True)  71.5 us
    unnamed x1, blocking collectives  10.6 us
    dot_general x1, matrix products, tile_pairs(): jnp.einsum('aie,bje->abij', own, other, preferred_element_type=jnp.float32)  7.94 us
    convert_element_type x1, other arithmetic, body(): (values / jnp.sqrt(jnp.sum(values * values, axis=2, keepdims=True) + 1e-0...  2.65 us
  transfers between devices with their start and end apart: 1, of which 1 were waited for; matrix products, arithmetic and copies ran while one was open for 2% of the time, Pallas kernels for 0%

commit v1 on v0

--- a/solution.py
+++ b/solution.py
@@ -1,7 +1,266 @@
+import functools
+
 import jax
 import jax.numpy as jnp
 from jax import lax
+from jax.experimental import pallas as pl
+from jax.experimental.pallas import tpu as pltpu
 from jax.sharding import PartitionSpec as P
+
+MESH = pl.DeviceIdType.MESH
+LOW = -4.0
+T = 128
+
+
+def kernel(chips, slots, len_ref, emb_ref, prec_ref, util_ref, units, relay, lens, rows, cols, res,
+           unit_in, relay_in, lens_in, res_in, send, side, pass_on, lens_out, res_out):
+    p, s = lax.axis_index("prompt"), lax.axis_index("sample")
+    x, y, z, c = p % 2, p // 2, s // 2, s % 2
+    flip = (x + y) % 2
+    hub_z = jnp.where(flip == 0, 2, 1)
+    v = jnp.where(flip == 0, z, chips - 1 - z)
+    across = jnp.where(c == 0, p + 1 - 2 * x, p + 2 - 4 * y)
+    chunks = units.shape[0]
+    is_hub = v == 2
+    is_near = v == 1
+    f32 = jnp.float32
+
+    def at(prompt, sample):
+        return {"prompt": prompt, "sample": sample}
+
+    def copy(src, dst, out_sem, in_sem, where):
+        return pltpu.make_async_remote_copy(
+            src_ref=src, dst_ref=dst, send_sem=out_sem, recv_sem=in_sem,
+            device_id=where, device_id_type=MESH)
+
+    barrier = pltpu.get_barrier_semaphore()
+
+    def greet(prompt, sample):
+        pl.semaphore_signal(barrier, inc=1, device_id=at(prompt, sample), device_id_type=MESH)
+
+    @pl.when(is_hub)
+    def _():
+        for d in range(1, slots):
+            greet(p, lax.rem(s + d, slots))
+        greet(across, s)
+        greet(across, 2 * (chips - 1 - z) + c)
+
+    @pl.when(jnp.logical_not(is_hub))
+    def _():
+        greet(p, 2 * hub_z)
+        greet(p, 2 * hub_z + 1)
+
+    @pl.when(is_near)
+    def _():
+        greet(across, s)
+
+    lens[s] = jnp.full(lens.shape[1:], len_ref[0], jnp.int32)
+
+    @pl.loop(0, chunks)
+    def _(k):
+        values = emb_ref[0, pl.ds(pl.multiple_of(k * T, T), T), :].astype(f32)
+        norm = jnp.sqrt(jnp.sum(values * values, axis=1, keepdims=True) + 1e-06)
+        units[k, s] = (values / norm).astype(units.dtype)
+
+    @pl.when(is_hub)
+    def _():
+        rows[...] = jnp.full(rows.shape, LOW, f32)
+        cols[...] = jnp.full(cols.shape, LOW, f32)
+        pl.semaphore_wait(barrier, slots + 1)
+
+    @pl.when(is_near)
+    def _():
+        pl.semaphore_wait(barrier, 3)
+
+    @pl.when(jnp.logical_not(is_hub | is_near))
+    def _():
+        pl.semaphore_wait(barrier, 2)
+
+    def own(k):
+        return units.at[k, s]
+
+    def straight(k):
+        return copy(own(k), own(k), send.at[k], unit_in.at[s, k], at(p, 2 * hub_z + c))
+
+    def detour(k):
+        return copy(own(k), relay.at[k], send.at[k], relay_in.at[k], at(across, s))
+
+    def hand_on(k):
+        return copy(relay.at[k], units.at[k, s], pass_on.at[k], unit_in.at[s, k],
+                    at(across, 2 * (chips - 1 - z) + c))
+
+    def to_side(k, slot):
+        return copy(units.at[k, slot], units.at[k, slot], side.at[slot, k], unit_in.at[slot, k],
+                    at(p, 2 * z + 1 - c))
+
+    def tell(core, where):
+        return copy(lens.at[s], lens.at[s], lens_out.at[core], lens_in.at[s], where)
+
+    far = jnp.logical_not(is_hub | is_near)
+
+    @pl.when(far)
+    def _():
+        for k in range(chunks):
+            straight(k).start()
+
+    @pl.when(is_near)
+    def _():
+        for k in range(chunks):
+            detour(k).start()
+
+    @pl.when(jnp.logical_not(is_hub))
+    def _():
+        for core in range(2):
+            tell(core, at(p, 2 * hub_z + core)).start()
+
+    @pl.when(is_hub)
+    def _():
+        tell(0, at(p, 2 * z + 1 - c)).start()
+        for k in range(chunks):
+            to_side(k, s).start()
+
+        def step(k):
+            return 2 * lax.rem(z + k, chips)
+
+        def others(k):
+            return [step(d) + c for d in range(1, chips)]
+
+        hand_wait = lambda k: copy(relay.at[k], relay.at[k], pass_on.at[k], relay_in.at[k],
+                                   at(p, 2 * z + 1 - c)).wait_recv()
+        hand_wait(0)
+        hand_on(0).start()
+        for d in range(1, slots):
+            other = lax.rem(s + d, slots)
+            copy(lens.at[other], lens.at[other], lens_out.at[0], lens_in.at[other],
+                 at(p, 2 * z + 1 - c)).wait_recv()
+
+        lane = lax.broadcasted_iota(jnp.int32, (1, T), 1)
+        lane8 = lax.broadcasted_iota(jnp.int32, (T, T), 1)
+        sub = lax.broadcasted_iota(jnp.int32, (T, T), 0)
+        high = f32(4.0)
+
+        def col_cap(k, slot):
+            return jnp.where(lane + k * T < lens[slot, 0:1, :], high, f32(LOW))
+
+        def row_cap(k, slot):
+            return jnp.where(sub + k * T < lens[slot, 0:1, :], high, f32(LOW))
+
+        def group(k, g):
+            return units[k, pl.ds(2 * g, 2)].reshape(2 * T, units.shape[3])
+
+        def against(k, g, h, js, keep):
+            new = group(k, g)
+            best = [[None, None], [None, None]]
+            caps = [row_cap(k, 2 * g + q) for q in range(2)]
+            for j in js:
+                similar = lax.dot_general(new, group(j, h), (((1,), (1,)), ((), ())),
+                                          preferred_element_type=f32)
+                for w in range(2):
+                    cap = col_cap(j, 2 * h + w)
+                    for q in range(2):
+                        part = similar[q * T:(q + 1) * T, w * T:(w + 1) * T]
+                        m = jnp.minimum(part, cap)
+                        best[q][w] = m if best[q][w] is None else jnp.maximum(best[q][w], m)
+                        if keep(j):
+                            n = jnp.max(jnp.minimum(part, caps[q]), axis=0, keepdims=True)
+                            at_row = (2 * h + w) * slots + 2 * g + q
+                            cols[j, pl.ds(at_row, 1), :] = jnp.maximum(cols[j, pl.ds(at_row, 1), :], n)
+            table = rows[k]
+            for q in range(2):
+                for w in range(2):
+                    top = jnp.max(best[q][w], axis=1, keepdims=True)
+                    table = jnp.where(lane8 == (2 * g + q) * slots + 2 * h + w, top, table)
+            rows[k] = table
+
+        for k in range(chunks):
+            if k + 1 < chunks:
+                hand_wait(k + 1)
+                hand_on(k + 1).start()
+            for slot in others(k):
+                to_side(k, slot).wait_recv()
+                to_side(k, slot).start()
+            for d in range(chips):
+                to_side(k, step(d) + 1 - c).wait_recv()
+
+            @pl.loop(0, chips - 1)
+            def _(i):
+                g = jnp.where(c == 0, i, lax.rem(3 * i + 2, chips + 1))
+                h = jnp.where(c == 0, i + 1, lax.rem(3 * i + 5, chips + 1))
+                against(k, g, h, range(k + 1), lambda j: True)
+                if k:
+                    against(k, h, g, range(k), lambda j: True)
+
+            @pl.loop(0, 2)
+            def _(i):
+                g = 2 * c + i
+                against(k, g, g, range(k + 1), lambda j: j < k)
+
+        pair = slots * slots
+        total = jnp.zeros((pair, 1), f32)
+        own_len = jnp.concatenate([lens[a] for a in range(slots)], axis=0)
+        for k in range(chunks):
+            best = jnp.maximum(rows[k].T[:pair], cols[k, :pair])
+            ok = (lax.broadcasted_iota(jnp.int32, (pair, T), 1) + k * T < own_len) & (best > -3.5)
+            total += jnp.sum(jnp.where(ok, best, f32(0.0)), axis=1, keepdims=True)
+        res[c] = total / own_len.astype(f32)
+        for d in range(1, slots):
+            copy(res.at[c], res.at[c], res_out.at[d], res_in.at[c], at(p, lax.rem(s + d, slots))).start()
+        for k in range(chunks):
+            hand_on(k).wait_send()
+            for d in range(chips):
+                to_side(k, step(d) + c).wait_send()
+        tell(0, at(p, 2 * z + 1 - c)).wait_send()
+        copy(res.at[1 - c], res.at[1 - c], res_out.at[0], res_in.at[1 - c], at(p, 2 * z + 1 - c)).wait_recv()
+
+    @pl.when(jnp.logical_not(is_hub))
+    def _():
+        for k in range(chunks):
+            straight(k).wait_send()
+        for core in range(2):
+            tell(core, at(p, 2 * hub_z + core)).wait_send()
+        for core in range(2):
+            copy(res.at[core], res.at[core], res_out.at[0], res_in.at[core],
+                 at(p, 2 * hub_z + core)).wait_recv()
+
+    whole = res[0] + res[1]
+    pair = slots * slots
+    index = lax.broadcasted_iota(jnp.int32, (pair, T), 0)
+    lanes = lax.broadcasted_iota(jnp.int32, (pair, T), 1)
+    row = jnp.sum(jnp.where(index == s * slots + lanes, whole, f32(0.0)), axis=0, keepdims=True)
+    prec_ref[...] = row[:, :slots]
+    first, second = index // slots, index % slots
+    mine = ((first == s) | (second == s)) & (first != second)
+    both = jnp.sum(jnp.where(mine, whole, f32(0.0)), axis=0, keepdims=True) / f32(2 * (slots - 1))
+    util_ref[...] = both[:, :1]
+
+    @pl.when(is_hub)
+    def _():
+        for d in range(1, slots):
+            copy(res.at[c], res.at[c], res_out.at[d], res_in.at[c], at(p, lax.rem(s + d, slots))).wait_send()
+
+
+def fused(slots, embeddings, lengths):
+    length, width = embeddings.shape[1:]
+    chunks = length // T
+    dma = pltpu.SemaphoreType.DMA
+    precision, utility = pl.pallas_call(
+        functools.partial(kernel, slots // 2, slots),
+        out_shape=(jax.ShapeDtypeStruct((1, slots), jnp.float32), jax.ShapeDtypeStruct((1, 1), jnp.float32)),
+        in_specs=[pl.BlockSpec(memory_space=pltpu.SMEM), pl.BlockSpec(memory_space=pltpu.VMEM)],
+        out_specs=(pl.BlockSpec(memory_space=pltpu.VMEM), pl.BlockSpec(memory_space=pltpu.VMEM)),
+        scratch_shapes=[
+            pltpu.VMEM((chunks, slots, T, width), jnp.bfloat16),
+            pltpu.VMEM((chunks, T, width), jnp.bfloat16),
+            pltpu.VMEM((slots, 8, T), jnp.int32),
+            pltpu.VMEM((chunks, T, T), jnp.float32),
+            pltpu.VMEM((chunks, slots * slots, T), jnp.float32),
+            pltpu.VMEM((2, slots * slots, T), jnp.float32),
+            dma((slots, chunks)), dma((chunks,)), dma((slots,)), dma((2,)),
+            dma((chunks,)), dma((slots, chunks)), dma((chunks,)), dma((2,)), dma((slots,)),
+        ],
+        compiler_params=pltpu.CompilerParams(collective_id=0, has_side_effects=True),
+    )(lengths, embeddings)
+    return precision, utility[:, 0]
 
 
 def tile_pairs(own, own_len, other, other_len):
@@ -43,4 +302,11 @@
 def solution(mesh):
     in_specs = (P(("prompt", "sample"), None, None), P(("prompt", "sample")))
     out_specs = (P(("prompt", "sample"), None), P(("prompt", "sample")))
-    return jax.shard_map(body, mesh=mesh, in_specs=in_specs, out_specs=out_specs, check_vma=False)
+
+    def run(embeddings, lengths):
+        slots = mesh.shape["sample"]
+        if mesh.shape["prompt"] == 4 and slots == 8 and embeddings.shape[0] == 1 and embeddings.shape[1] % T == 0:
+            return fused(slots, embeddings, lengths)
+        return body(embeddings, lengths)
+
+    return jax.shard_map(run, mesh=mesh, in_specs=in_specs, out_specs=out_specs, check_vma=False)

time: 114 us -> 68.7 us (0.60)
  waiting for transfers between devices: 71.5 us -> 0 us
  Pallas kernels: 0 us -> 64.3 us
  between operations: 16.5 us -> 3.05 us
  blocking collectives: 10.6 us -> 0 us
  matrix products: 7.94 us -> 0 us
  other arithmetic: 5.55 us -> 0 us
    all_gather x1 -> x0, waiting for transfers between devices: 71.5 us -> none  [body(): piece = lax.all_gather(unit, 'sample', axis=0, tiled=True)]
    pallas_call x0 -> x1, Pallas kernels: none -> 64.3 us  [fused(): pl.pallas_call(functools.partial(kernel, slots // 2, slots), out_shape=(j...]
    unnamed x1 -> x0, blocking collectives: 10.6 us -> none
    dot_general x1 -> x0, matrix products: 7.94 us -> none  [tile_pairs(): jnp.einsum('aie,bje->abij', own, other, preferred_element_type=jnp.float32)]
    reduce_sum x3 -> x0, other arithmetic: 2.81 us -> none  [the longest x1 1.5 us: body(): jnp.sum(values * values, axis=2, keepdims=True) + 1e-06]
    convert_element_type x1 -> x0, other arithmetic: 2.65 us -> none  [body(): (values / jnp.sqrt(jnp.sum(values * values, axis=2, keepdims=True) + 1e-0...]
  transfers between devices with their start and end apart: 1 -> 0, of which waited for: 1 -> 0; matrix products, arithmetic and copies ran while one was open for 2% -> 0% of each run, Pallas kernels for 0% -> 0%
where the time goes in v1:
time: 68.7 us; the launch traced here: 68.5 us
  Pallas kernels  64.3 us (94%)
  between operations  3.05 us (4%)
  local copies, waits for them, and re-layouts  1.13 us (2%)
    pallas_call x1, Pallas kernels, fused(): pl.pallas_call(functools.partial(kernel, slots // 2, slots), out_shape=(j...  64.3 us

profile of v1, /device:TPU:0, one launch (start us, length us, event | category | flops | bytes accessed | tf_op | source)
XLA Modules:
  0.0 68.5 jit_solution(18038177018829698999)
XLA Ops:
  1.3 64.3 %shard_map.41 = (f32[1,8]{1,0:T(1,128)}, f32[1,1]{1,0:T(1,128)}) custom-call(s32[1]{0:T(128)S(6)} %copy.6.len_ref, bf16[1,512,1024]{2,1,0:T(8,128)(2,1)} %emb_ref.1), custom_call_target="tpu_custom_call" | custom-call | tf_op jit(solution)/shard_map/pallas_call | solution.py:246
  65.6 0.0 copy-start
  65.6 0.6 copy-done
  66.2 0.5 copy.7
Async XLA Ops:
  65.6 0.6 copy-start

commit v2 on v1

--- a/solution.py
+++ b/solution.py
@@ -127,8 +127,9 @@
 
         hand_wait = lambda k: copy(relay.at[k], relay.at[k], pass_on.at[k], relay_in.at[k],
                                    at(p, 2 * z + 1 - c)).wait_recv()
-        hand_wait(0)
-        hand_on(0).start()
+        for k in range(3):
+            hand_wait(k)
+            hand_on(k).start()
         for d in range(1, slots):
             other = lax.rem(s + d, slots)
             copy(lens.at[other], lens.at[other], lens_out.at[0], lens_in.at[other],
@@ -173,16 +174,16 @@
             rows[k] = table
 
         for k in range(chunks):
-            if k + 1 < chunks:
-                hand_wait(k + 1)
-                hand_on(k + 1).start()
+            if k + 3 < chunks:
+                hand_wait(k + 3)
+                hand_on(k + 3).start()
             for slot in others(k):
                 to_side(k, slot).wait_recv()
                 to_side(k, slot).start()
             for d in range(chips):
                 to_side(k, step(d) + 1 - c).wait_recv()
 
-            @pl.loop(0, chips - 1)
+            @pl.loop(0, chips - 1, unroll=True)
             def _(i):
                 g = jnp.where(c == 0, i, lax.rem(3 * i + 2, chips + 1))
                 h = jnp.where(c == 0, i + 1, lax.rem(3 * i + 5, chips + 1))
@@ -190,7 +191,7 @@
                 if k:
                     against(k, h, g, range(k), lambda j: True)
 
-            @pl.loop(0, 2)
+            @pl.loop(0, 2, unroll=True)
             def _(i):
                 g = 2 * c + i
                 against(k, g, g, range(k + 1), lambda j: j < k)
@@ -202,7 +203,10 @@
             best = jnp.maximum(rows[k].T[:pair], cols[k, :pair])
             ok = (lax.broadcasted_iota(jnp.int32, (pair, T), 1) + k * T < own_len) & (best > -3.5)
             total += jnp.sum(jnp.where(ok, best, f32(0.0)), axis=1, keepdims=True)
-        res[c] = total / own_len.astype(f32)
+        share = total / own_len.astype(f32)
+        place = lax.broadcasted_iota(jnp.int32, (pair, T), 0) % slots
+        spread = jnp.where(lax.broadcasted_iota(jnp.int32, (pair, T), 1) == place, share, f32(0.0))
+        res[c] = jnp.sum(spread.reshape(slots, slots, T), axis=1)
         for d in range(1, slots):
             copy(res.at[c], res.at[c], res_out.at[d], res_in.at[c], at(p, lax.rem(s + d, slots))).start()
         for k in range(chunks):
@@ -223,15 +227,13 @@
                  at(p, 2 * hub_z + core)).wait_recv()
 
     whole = res[0] + res[1]
-    pair = slots * slots
-    index = lax.broadcasted_iota(jnp.int32, (pair, T), 0)
-    lanes = lax.broadcasted_iota(jnp.int32, (pair, T), 1)
-    row = jnp.sum(jnp.where(index == s * slots + lanes, whole, f32(0.0)), axis=0, keepdims=True)
+    first = lax.broadcasted_iota(jnp.int32, (slots, T), 0)
+    second = lax.broadcasted_iota(jnp.int32, (slots, T), 1)
+    row = jnp.sum(jnp.where(first == s, whole, f32(0.0)), axis=0, keepdims=True)
     prec_ref[...] = row[:, :slots]
-    first, second = index // slots, index % slots
     mine = ((first == s) | (second == s)) & (first != second)
-    both = jnp.sum(jnp.where(mine, whole, f32(0.0)), axis=0, keepdims=True) / f32(2 * (slots - 1))
-    util_ref[...] = both[:, :1]
+    both = jnp.sum(jnp.where(mine, whole, f32(0.0)), axis=0, keepdims=True)
+    util_ref[...] = jnp.sum(both, axis=1, keepdims=True) / f32(2 * (slots - 1))
 
     @pl.when(is_hub)
     def _():
@@ -254,7 +256,7 @@
             pltpu.VMEM((slots, 8, T), jnp.int32),
             pltpu.VMEM((chunks, T, T), jnp.float32),
             pltpu.VMEM((chunks, slots * slots, T), jnp.float32),
-            pltpu.VMEM((2, slots * slots, T), jnp.float32),
+            pltpu.VMEM((2, slots, T), jnp.float32),
             dma((slots, chunks)), dma((chunks,)), dma((slots,)), dma((2,)),
             dma((chunks,)), dma((slots, chunks)), dma((chunks,)), dma((2,)), dma((slots,)),
         ],

time: 68.7 us -> 59 us (0.86)
  Pallas kernels: 64.3 us -> 54.6 us
    pallas_call x1, Pallas kernels: 64.3 us -> 54.6 us  [fused(): pl.pallas_call(functools.partial(kernel, slots // 2, slots), out_shape=(j...]
where the time goes in v2:
time: 59 us; the launch traced here: 58.8 us
  Pallas kernels  54.6 us (93%)
  between operations  3.05 us (5%)
  local copies, waits for them, and re-layouts  1.13 us (2%)
    pallas_call x1, Pallas kernels, fused(): pl.pallas_call(functools.partial(kernel, slots // 2, slots), out_shape=(j...  54.6 us

profile of v2, /device:TPU:0, one launch (start us, length us, event | category | flops | bytes accessed | tf_op | source)
XLA Modules:
  0.0 58.8 jit_solution(6143057738111564582)
XLA Ops:
  1.3 54.6 %shard_map.41 = (f32[1,8]{1,0:T(1,128)}, f32[1,1]{1,0:T(1,128)}) custom-call(s32[1]{0:T(128)S(6)} %copy.6.len_ref, bf16[1,512,1024]{2,1,0:T(8,128)(2,1)} %emb_ref.1), custom_call_target="tpu_custom_call" | custom-call | tf_op jit(solution)/shard_map/pallas_call | solution.py:248
  55.9 0.0 copy-start
  55.9 0.6 %copy-done = f32[1,8]{1,0:T(1,128)S(1)} copy-done((f32[1,8]{1,0:T(1,128)S(1)}, f32[1,8]{1,0:T(1,128)}, u32[]{:S(2)}) %copy-start) | copy-done | bytes 56
  56.5 0.5 copy.7
Async XLA Ops:
  55.9 0.6 %copy-start = (f32[1,8]{1,0:T(1,128)S(1)}, f32[1,8]{1,0:T(1,128)}, u32[]{:S(2)}) copy-start(f32[1,8]{1,0:T(1,128)} %get-tuple-element.8) | copy-start | bytes 100

commit v3 on v2

--- a/solution.py
+++ b/solution.py
@@ -127,7 +127,7 @@
 
         hand_wait = lambda k: copy(relay.at[k], relay.at[k], pass_on.at[k], relay_in.at[k],
                                    at(p, 2 * z + 1 - c)).wait_recv()
-        for k in range(3):
+        for k in range(chunks):
             hand_wait(k)
             hand_on(k).start()
         for d in range(1, slots):
@@ -173,13 +173,15 @@
                     table = jnp.where(lane8 == (2 * g + q) * slots + 2 * h + w, top, table)
             rows[k] = table
 
-        for k in range(chunks):
-            if k + 3 < chunks:
-                hand_wait(k + 3)
-                hand_on(k + 3).start()
+        def share_out(k):
             for slot in others(k):
                 to_side(k, slot).wait_recv()
                 to_side(k, slot).start()
+
+        share_out(0)
+        for k in range(chunks):
+            if k + 1 < chunks:
+                share_out(k + 1)
             for d in range(chips):
                 to_side(k, step(d) + 1 - c).wait_recv()
 

time: 59 us -> 52.9 us (0.90)
  Pallas kernels: 54.6 us -> 48.5 us
    pallas_call x1, Pallas kernels: 54.6 us -> 48.5 us  [fused(): pl.pallas_call(functools.partial(kernel, slots // 2, slots), out_shape=(j...]
where the time goes in v3:
time: 52.9 us; the launch traced here: 52.7 us
  Pallas kernels  48.5 us (92%)
  between operations  3.05 us (6%)
  local copies, waits for them, and re-layouts  1.13 us (2%)
    pallas_call x1, Pallas kernels, fused(): pl.pallas_call(functools.partial(kernel, slots // 2, slots), out_shape=(j...  48.5 us
    unnamed x3, local copies, waits for them, and re-layouts  1.13 us

profile of v3, /device:TPU:0, one launch (start us, length us, event | category | flops | bytes accessed | tf_op | source)
XLA Modules:
  0.0 52.7 jit_solution(15796290046690470150)
XLA Ops:
  1.3 48.5 %shard_map.41 = (f32[1,8]{1,0:T(1,128)}, f32[1,1]{1,0:T(1,128)}) custom-call(s32[1]{0:T(128)S(6)} %copy.6.len_ref, bf16[1,512,1024]{2,1,0:T(8,128)(2,1)} %emb_ref.1), custom_call_target="tpu_custom_call" | custom-call | tf_op jit(solution)/shard_map/pallas_call | solution.py:250
  49.8 0.0 copy-start
  49.8 0.6 %copy-done = f32[1,8]{1,0:T(1,128)S(1)} copy-done((f32[1,8]{1,0:T(1,128)S(1)}, f32[1,8]{1,0:T(1,128)}, u32[]{:S(2)}) %copy-start) | copy-done | bytes 56
  50.4 0.5 copy.7
Async XLA Ops:
  49.8 0.6 %copy-start = (f32[1,8]{1,0:T(1,128)S(1)}, f32[1,8]{1,0:T(1,128)}, u32[]{:S(2)}) copy-start(f32[1,8]{1,0:T(1,128)} %get-tuple-element.8) | copy-start | bytes 100
